TPU v7x, 32 devices: a whole 2x2x4 slice. The times are simulated.
32 devices in a mesh: dp: 4 (over z), fsdp: 8 (over y, x, core).
Axes of the slice: x: 2, y: 2, z: 4, core: 2. Of those that a mesh axis runs over, the one named last changes fastest.
Arguments:
- frames: bfloat16 [64, 256, 1536], P(('dp', 'fsdp')), may hold values from -6 to 6
- lengths: int32 [64], P(('dp', 'fsdp')), may hold values from 1 to 256, as said below
- norm_in_gain: float32 [1536], replicated, may hold values from 0.1 to 1.9
- w_in: bfloat16 [1536, 3072], P('fsdp'), may hold values from -0.15625 to 0.15625
- dw_kernel: float32 [31, 1536], replicated, may hold values from -1 to 1
- norm_mid_gain: float32 [1536], replicated, may hold values from 0.1 to 1.9
- w_out: bfloat16 [1536, 1536], P('fsdp'), may hold values from -0.15625 to 0.15625
Outputs:
- module_out: bfloat16 [64, 256, 1536], P(('dp', 'fsdp'))
Inputs may be any that keep to these rules, and one draw needn't show every extreme that they name: Utterance u has ceil(lengths[u] / 64) live blocks. Two devices of the same dp index whose fsdp indices differ by half of 8 hold at most 10 live blocks together; in every dp group some such pair holds exactly 10, one device of it having all 8 blocks live with every utterance of length 256.
All inputs are finite; a program needn't handle non-finite values.
Results may differ from a plain program's by a relative error of at most 0.0066.
Values may be sent and summed in bfloat16 or wider, within the bound.
A program may use at most 128 MiB of HBM per device.

v0:
```python
import jax
import jax.numpy as jnp
from jax import lax
from jax.sharding import PartitionSpec as P


def layer_norm(values, gain_vec):
    center = values - jnp.mean(values, axis=-1, keepdims=True)
    spread = jnp.mean(center * center, axis=-1, keepdims=True)
    return center * lax.rsqrt(spread + 1e-05) * gain_vec


def expand_in(flat_rows, w_in):
    model_width = flat_rows.shape[1]
    projected = jnp.dot(
        flat_rows,
        lax.all_gather(w_in, "fsdp", axis=0, tiled=True),
        preferred_element_type=jnp.float32,
    )
    return (projected[:, :model_width] * jax.nn.sigmoid(projected[:, model_width:])).astype(
        jnp.bfloat16
    )


def contract_out(flat_rows, w_out):
    projected = jnp.dot(
        flat_rows,
        lax.all_gather(w_out, "fsdp", axis=0, tiled=True),
        preferred_element_type=jnp.float32,
    )
    return projected.astype(jnp.bfloat16)


def on_device(frames, lengths, norm_in_gain, w_in, dw_kernel, norm_mid_gain, w_out):
    utt_count, frame_span, model_width = frames.shape
    positions = jnp.arange(frame_span, dtype=jnp.int32)
    valid = (positions[None, :] < lengths[:, None])[:, :, None]
    normed = layer_norm(frames.astype(jnp.float32), norm_in_gain).astype(jnp.bfloat16)

    def apply_rows(values, compute):
        return compute(values.reshape(utt_count * frame_span, model_width)).reshape(
            utt_count, frame_span, -1
        )

    def first_section(flat_rows):
        return expand_in(flat_rows, w_in)

    def last_section(flat_rows):
        return contract_out(flat_rows, w_out)

    gated = apply_rows(normed, first_section)
    gated = jnp.where(valid, gated, jnp.zeros((), jnp.bfloat16))
    taps = dw_kernel.shape[0]
    half_k = (taps - 1) // 2
    padded = jnp.pad(gated, ((0, 0), (half_k, half_k), (0, 0)))
    convolved = jnp.zeros((utt_count, frame_span, model_width), jnp.float32)
    for offset in range(taps):
        convolved = convolved + padded[:, offset : offset + frame_span, :] * dw_kernel[offset]
    middle = layer_norm(convolved, norm_mid_gain)
    middle = (middle * jax.nn.sigmoid(middle)).astype(jnp.bfloat16)
    result = apply_rows(middle, last_section)
    return jnp.where(valid, result, jnp.zeros((), jnp.bfloat16))


def solution(mesh):
    return jax.shard_map(
        on_device,
        mesh=mesh,
        in_specs=(
            P(("dp", "fsdp"), None, None),
            P(("dp", "fsdp")),
            P(),
            P("fsdp", None),
            P(),
            P(),
            P("fsdp", None),
        ),
        out_specs=P(("dp", "fsdp"), None, None),
        check_vma=False,
    )
```

profile of v0, /device:TPU:0, one launch (start us, length us, event | category | flops | bytes accessed | tf_op | source)
XLA Modules:
  0.0 124.5 jit_solution(6595838935682310830)
XLA Ops:
  6.5 0.0 copy-start
  6.5 0.0 copy-start.3
  6.5 0.0 copy-start.1
  6.5 0.0 all-gather.3.cloned.1.call-start
  6.5 0.7 all-gather.3.cloned.1.call-update
  7.3 0.0 all-gather.5.cloned.1.call-start
  7.3 0.7 all-gather.5.cloned.1.call-update
  8.0 1.5 %slice_reduce_fusion.29 = (f32[1536]{0:T(1024)S(1)}, f32[1536]{0:T(1024)S(1)}, f32[1536]{0:T(1024)S(1)}, f32[1536]{0:T(1024)S(1)}, f32[1536]{0:T(1024)S(1)}, /*i...) fusion(f32[31,1536]{1,0:T(8,128)} %param.11), kind=kLoop, calls=%fused_computation.56 | loop fusion | bytes 147456 | tf_op jit(solution)/shard_map/slice | solution.py:58
  9.5 2.1 %slice_reduce_fusion.30 = (f32[1536]{0:T(1024)S(1)}, f32[1536]{0:T(1024)S(1)}, f32[1536]{0:T(1024)S(1)}, f32[1536]{0:T(1024)S(1)}, f32[1536]{0:T(1024)S(1)}, /*i...) fusion(f32[31,1536]{1,0:T(8,128)} %param.11), kind=kLoop, calls=%fused_computation.57 | loop fusion | bytes 233472 | tf_op jit(solution)/shard_map/slice | solution.py:58
  11.6 0.0 copy-done
  11.6 0.3 convert_reduce_fusion
  11.9 0.0 copy-done.3
  11.9 0.1 iota_compare_fusion
  12.0 0.6 fusion.2
  12.5 0.0 copy-done.1
  12.5 0.5 fusion.4
  13.1 57.6 %all-gather.3.cloned.1.call-done = bf16[1536,3072]{1,0:T(8,128)(2,1)} async-done(((bf16[192,3072]{1,0:T(8,128)(2,1)}), bf16[1536,3072]{1,0:T(8,128)(2,1)}) %all-gather.3.cloned.1.call-update) | async-done | bytes 9437200 | tf_op jit(solution)/shard_map/all_gather | solution.py:17
  70.7 7.6 %fusion.11 = f32[512,3072]{1,0:T(8,128)S(1)} fusion(bf16[512,1536]{1,0:T(8,128)(2,1)S(1)} %bitcast.9, bf16[1536,3072]{1,0:T(8,128)(2,1)} %all-gather.3.cloned.1.call-done), kind=kOutput, calls=%fused_computation.64 | convolution fusion | flops 4831838208 | bytes 17301504 | tf_op jit(solution)/shard_map/dot_general | solution.py:15
  78.3 0.8 fusion.9
  79.1 0.2 broadcast_select_fusion.1
  79.3 0.0 copy-start.2
  79.3 13.8 %fusion.10 = (f32[2,256]{1,0:T(2,128)S(1)}, f32[2,256,1536]{2,1,0:T(8,128)S(1)}) fusion(f32[1536]{0:T(1024)S(1)} %get-tuple-element.34, f32[1536]{0:T(1024)S(1)} %get-tuple-element.35, f32[1536]{0:T(1024)S(1)} %get-tuple-element.6, f32[1536]{0:T(1024)S(1)} %get-tuple-element.7, f32[1536]{0:T(1024)S(1)} %get-tuple-element.8, f32[1536]{0:T(1024)S(1)} %get-tuple-element.9, ...), kind=kLoop, calls=%fused_computation.63 | loop fusion | flops 73137664 | bytes 4911104 | tf_op jit(solution)/shard_map/reduce_sum | solution.py:8
  93.1 0.5 multiply_reduce_fusion
  93.5 0.0 copy-done.2
  93.6 1.1 multiply_convert_fusion
  94.6 16.7 %all-gather.5.cloned.1.call-done = bf16[1536,1536]{1,0:T(8,128)(2,1)} async-done(((bf16[192,1536]{1,0:T(8,128)(2,1)}), bf16[1536,1536]{1,0:T(8,128)(2,1)}) %all-gather.5.cloned.1.call-update) | async-done | bytes 4718608 | tf_op jit(solution)/shard_map/all_gather | solution.py:28
  111.4 5.0 %convolution_convert_fusion = bf16[512,1536]{1,0:T(8,128)(2,1)S(1)} fusion(bf16[512,1536]{1,0:T(8,128)(2,1)S(1)} %bitcast.11, bf16[1536,1536]{1,0:T(8,128)(2,1)} %all-gather.5.cloned.1.call-done), kind=kOutput, calls=%fused_computation.16 | convolution fusion | flops 2416705536 | bytes 7864320 | tf_op jit(solution)/shard_map/dot_general | solution.py:26
  116.3 1.3 %broadcast_select_fusion = bf16[2,256,1536]{2,1,0:T(8,128)(2,1)} fusion(bf16[2,256,1536]{2,1,0:T(8,128)(2,1)S(1)} %bitcast.10, pred[2,256]{1,0:T(4,128)(4,1)S(1)} %iota_compare_fusion), kind=kLoop, calls=%fused_computation.25 | loop fusion | flops 786432 | bytes 3146240 | tf_op jit(solution)/shard_map/jit(_where)/select_n | solution.py:62
  (4 shorter events, 0.0 us)
Async XLA Ops:
  6.5 5.1 %copy-start = (bf16[2,256,1536]{2,1,0:T(8,128)(2,1)S(1)}, bf16[2,256,1536]{2,1,0:T(8,128)(2,1)}, u32[]{:S(2)}) copy-start(bf16[2,256,1536]{2,1,0:T(8,128)(2,1)} %param.7) | copy-start | bytes 4718596
  6.5 5.3 %copy-start.3 = (s32[2]{0:T(128)S(1)}, s32[2]{0:T(128)}, u32[]{:S(2)}) copy-start(s32[2]{0:T(128)} %param.8) | copy-start | bytes 28
  6.5 6.0 %copy-start.1 = (f32[1536]{0:T(1024)S(1)}, f32[1536]{0:T(1024)}, u32[]{:S(2)}) copy-start(f32[1536]{0:T(1024)} %param.9) | copy-start | bytes 18436
  6.5 64.1 %all-gather.3.cloned.1.call-start = ((), (), s32[]{:S(2)}) async-start(), calls=%async_computation | async-start | bytes 10616832 | tf_op jit(solution)/shard_map/all_gather | solution.py:17
  7.3 104.1 %all-gather.5.cloned.1.call-start = ((), (), s32[]{:S(2)}) async-start(), calls=%async_computation.1 | async-start | bytes 5308416 | tf_op jit(solution)/shard_map/all_gather | solution.py:28
  79.3 14.3 %copy-start.2 = (f32[1536]{0:T(1024)S(1)}, f32[1536]{0:T(1024)}, u32[]{:S(2)}) copy-start(f32[1536]{0:T(1024)} %param.12) | copy-start | bytes 18436
Sparse Core Ops, SparseCore 0:
  9.2 61.4 all-gather.2
  72.6 38.7 all-gather.4
where the time goes:
time: 125 us; the launch traced here: 124 us
  waiting for transfers between devices  75.7 us (61%)
  other arithmetic  19.1 us (15%)
  between operations  13.5 us (11%)
  matrix products  12.5 us (10%)
  local copies, waits for them, and re-layouts  3.59 us (3%)
    all_gather x1, waiting for transfers between devices, expand_in(): lax.all_gather(w_in, 'fsdp', axis=0, tiled=True)  57.6 us
    all_gather x1, waiting for transfers between devices, contract_out(): lax.all_gather(w_out, 'fsdp', axis=0, tiled=True)  16.7 us
    reduce_sum x2, other arithmetic, layer_norm(): center = values - jnp.mean(values, axis=-1, keepdims=True)  14.1 us
    dot_general x1, matrix products, expand_in(): jnp.dot(flat_rows, lax.all_gather(w_in, 'fsdp', axis=0, tiled=True), pref...  7.59 us
    dot_general x1, matrix products, contract_out(): jnp.dot(flat_rows, lax.all_gather(w_out, 'fsdp', axis=0, tiled=True), pre...  4.95 us
    slice x2, local copies, waits for them, and re-layouts, on_device(): dw_kernel[offset]  3.57 us
  transfers between devices with their start and end apart: 2, of which 2 were waited for; matrix products, arithmetic and copies ran while one was open for 23% of the time, Pallas kernels for 0%

commit v1 on v0

--- a/solution.py
+++ b/solution.py
@@ -1,6 +1,8 @@
 import jax
 import jax.numpy as jnp
 from jax import lax
+from jax.experimental import pallas as pl
+from jax.experimental.pallas import tpu as pltpu
 from jax.sharding import PartitionSpec as P
 
 
@@ -62,9 +64,264 @@
     return jnp.where(valid, result, jnp.zeros((), jnp.bfloat16))
 
 
+MESH = pl.DeviceIdType.MESH
+WIDE = 512
+HALO = 16
+TILE = 64
+
+
+def fused_kernel(
+    lengths, frames, gain_in, w_in, taps, gain_mid, w_out,
+    out, wbuf, normed, gated, conv, middle, load_sem, send_sem, recv_sem
+):
+    utts, span, width = frames.shape
+    rows = w_in.shape[0]
+    half = rows // 2
+    cw = WIDE // 2
+    n_taps = taps.shape[0]
+    me = lax.axis_index("fsdp")
+    dp = lax.axis_index("dp")
+    par = lax.rem(dp, 2)
+    core = lax.rem(me, 2)
+    bit_x = lax.rem(me // 2, 2)
+    bit_y = lax.rem(me // 4, 2)
+    fx = me + 2 - 4 * bit_x
+    fy = me + 4 - 8 * bit_y
+    fxy = fx + 4 - 8 * bit_y
+    fc = me + 1 - 2 * core
+    to_x, to_y, to_c = {"fsdp": fx}, {"fsdp": fy}, {"fsdp": fc}
+    to_z = {"dp": dp + 1 - 2 * par}
+    n_in = width // cw
+    n_all = n_in + width // WIDE
+
+    def chunk(slot):
+        g, r = slot // 3, slot % 3
+        return 3 * g + (par if r == 0 else 1 - par if r == 1 else 2)
+
+    def block(slot, owner, start=0, count=rows):
+        first = pl.multiple_of(owner * rows + start, 16)
+        return wbuf.at[chunk(slot), pl.ds(first, count), :]
+
+    started = []
+
+    def send(slot, kind, owner, target, start=0, count=rows):
+        ref = block(slot, owner, start, count)
+        copy = pltpu.make_async_remote_copy(
+            src_ref=ref, dst_ref=ref,
+            send_sem=send_sem.at[slot, kind], recv_sem=recv_sem.at[slot, kind],
+            device_id=target, device_id_type=MESH,
+        )
+        copy.start()
+        started.append(copy)
+
+    def arrived(slot, kind, owner, start=0, count=rows, sem_slot=None):
+        ref = block(slot, owner, start, count)
+        sem = slot if sem_slot is None else sem_slot
+        pltpu.make_async_remote_copy(
+            src_ref=ref, dst_ref=ref,
+            send_sem=send_sem.at[sem, kind], recv_sem=recv_sem.at[sem, kind],
+            device_id=to_c, device_id_type=MESH,
+        ).wait_recv()
+
+    X, Y, RX, RY, C0, CX, CY, CD, ZX, ZY, ZD = range(11)
+
+    def load_copies(slot):
+        j = chunk(slot)
+        own = pl.ds(pl.multiple_of(me * rows, 16), rows)
+        if slot < n_in:
+            lo = pl.multiple_of(j * cw, cw)
+            return [
+                pltpu.make_async_copy(
+                    w_in.at[:, pl.ds(lo, cw)], wbuf.at[j, own, pl.ds(0, cw)],
+                    load_sem.at[slot, 0]),
+                pltpu.make_async_copy(
+                    w_in.at[:, pl.ds(lo + width, cw)], wbuf.at[j, own, pl.ds(cw, cw)],
+                    load_sem.at[slot, 1]),
+            ]
+        lo = pl.multiple_of((j - n_in) * WIDE, WIDE)
+        return [
+            pltpu.make_async_copy(
+                w_out.at[:, pl.ds(lo, WIDE)], wbuf.at[j, own, :], load_sem.at[slot, 0])
+        ]
+
+    def own(slot):
+        for copy in load_copies(slot):
+            copy.wait()
+        if slot % 3 != 1:
+            send(slot, X, me, to_x)
+            send(slot, Y, me, to_y)
+        send(slot, C0, me, to_c)
+
+    def relay(slot):
+        arrived(slot, X, fx)
+        send(slot, RY, fx, to_y, 0, half)
+        if slot % 3 == 0:
+            send(slot, ZX, fx, to_z)
+        send(slot, CX, fx, to_c)
+        arrived(slot, Y, fy)
+        send(slot, RX, fy, to_x, half, half)
+        if slot % 3 == 0:
+            send(slot, ZY, fy, to_z)
+        send(slot, CY, fy, to_c)
+
+    def finish(slot):
+        arrived(slot, RY, fxy, 0, half)
+        arrived(slot, RX, fxy, half, half)
+        if slot % 3 == 0:
+            send(slot, ZD, fxy, to_z)
+        send(slot, CD, fxy, to_c)
+
+    def from_z(slot):
+        for z_kind, c_kind, owner in ((ZX, CX, fx), (ZY, CY, fy), (ZD, CD, fxy)):
+            arrived(slot, z_kind, owner, sem_slot=slot - 1)
+            send(slot, c_kind, owner, to_c)
+
+    def ready(slot):
+        for kind, owner in ((C0, me), (CX, fx), (CY, fy), (CD, fxy)):
+            arrived(slot, kind, owner + 1 - 2 * core)
+
+    def norm_in():
+        for u in range(utts):
+            @pl.loop(0, span // TILE)
+            def _(t):
+                at = pl.ds(pl.multiple_of(t * TILE, TILE), TILE)
+                v = frames[u, at, :].astype(jnp.float32)
+                v = v - jnp.mean(v, axis=-1, keepdims=True)
+                var = jnp.mean(v * v, axis=-1, keepdims=True)
+                v = v * lax.rsqrt(var + 1e-05) * gain_in[...]
+                normed[u, at, :] = v.astype(jnp.bfloat16)
+
+    def project(slot):
+        ready(slot)
+        j = chunk(slot)
+        for u in range(utts):
+            acc = jnp.dot(normed[u], wbuf[j], preferred_element_type=jnp.float32)
+            value = acc[:, :cw] * jax.nn.sigmoid(acc[:, cw:])
+            pos = lax.broadcasted_iota(jnp.int32, (span, cw), 0)
+            value = jnp.where(pos < lengths[u], value, 0.0)
+            value = value.astype(jnp.bfloat16).astype(jnp.float32)
+            for lane in range(cw // 128):
+                gated[lane, u, HALO:HALO + span, :] = value[:, lane * 128:(lane + 1) * 128]
+        for lane in range(cw // 128):
+            k_at = pl.ds(pl.multiple_of(j * cw + lane * 128, 128), 128)
+            for u in range(utts):
+                @pl.loop(0, span // TILE)
+                def _(t):
+                    first = pl.multiple_of(t * TILE, TILE)
+                    total = jnp.zeros((TILE, 128), jnp.float32)
+                    for k in range(n_taps):
+                        shift = HALO - (n_taps - 1) // 2 + k
+                        total = total + gated[lane, u, pl.ds(first + shift, TILE), :] * taps[k:k + 1, k_at]
+                    conv[j, u, pl.ds(first, TILE), lane * 128:(lane + 1) * 128] = total
+
+    def norm_mid():
+        for u in range(utts):
+            @pl.loop(0, span // 32)
+            def _(t):
+                at = pl.ds(pl.multiple_of(t * 32, 32), 32)
+                parts = [conv[j, u, at, :] for j in range(n_in)]
+                mean = sum(jnp.sum(p, axis=-1, keepdims=True) for p in parts) / width
+                parts = [p - mean for p in parts]
+                var = sum(jnp.sum(p * p, axis=-1, keepdims=True) for p in parts) / width
+                scale = lax.rsqrt(var + 1e-05)
+                for j, p in enumerate(parts):
+                    v = p * scale * gain_mid[:, j * cw:(j + 1) * cw]
+                    v = v * jax.nn.sigmoid(v)
+                    middle[u, at, j * cw:(j + 1) * cw] = v.astype(jnp.bfloat16)
+
+    def contract(slot):
+        ready(slot)
+        j = chunk(slot)
+        to = pl.ds(pl.multiple_of((j - n_in) * WIDE, WIDE), WIDE)
+        for u in range(utts):
+            acc = jnp.dot(middle[u], wbuf[j], preferred_element_type=jnp.float32)
+            pos = lax.broadcasted_iota(jnp.int32, (span, WIDE), 0)
+            out[u, :, to] = jnp.where(pos < lengths[u], acc, 0.0).astype(jnp.bfloat16)
+
+    m0, o0, s0, m1, o1, s1, m2, o2, s2 = range(n_all)
+    for slot in (m0, s0, m1, o0, s1, m2, o1, s2, o2):
+        for copy in load_copies(slot):
+            copy.start()
+    barrier = pltpu.get_barrier_semaphore()
+    for target in (to_x, to_y, to_c, to_z):
+        pl.semaphore_signal(barrier, inc=1, device_id=target, device_id_type=MESH)
+    pl.semaphore_wait(barrier, 4)
+
+    own(m0)
+    for lane in range(cw // 128):
+        for u in range(utts):
+            gated[lane, u, :HALO, :] = jnp.zeros((HALO, 128), jnp.float32)
+            gated[lane, u, HALO + span:, :] = jnp.zeros((HALO, 128), jnp.float32)
+    norm_in()
+    relay(m0)
+    own(s0)
+    finish(m0)
+    own(m1)
+    own(o0)
+    project(m0)
+    relay(s0)
+    own(s1)
+    relay(m1)
+    own(m2)
+    finish(s0)
+    project(s0)
+    from_z(o0)
+    finish(m1)
+    project(o0)
+    relay(s1)
+    own(s2)
+    own(o1)
+    own(o2)
+    project(m1)
+    relay(m2)
+    finish(s1)
+    project(s1)
+    from_z(o1)
+    relay(s2)
+    finish(m2)
+    project(o1)
+    finish(s2)
+    norm_mid()
+    contract(m2)
+    contract(s2)
+    from_z(o2)
+    contract(o2)
+    for copy in started:
+        copy.wait_send()
+
+
+def fused_device(frames, lengths, norm_in_gain, w_in, dw_kernel, norm_mid_gain, w_out):
+    utts, span, width = frames.shape
+    n_in = width // (WIDE // 2)
+    n_all = n_in + width // WIDE
+    vmem = pl.BlockSpec(memory_space=pltpu.VMEM)
+    hbm = pl.BlockSpec(memory_space=pl.ANY)
+    return pl.pallas_call(
+        fused_kernel,
+        out_shape=jax.ShapeDtypeStruct(frames.shape, jnp.bfloat16),
+        in_specs=[pl.BlockSpec(memory_space=pltpu.SMEM), vmem, vmem, hbm, vmem, vmem, hbm],
+        out_specs=vmem,
+        scratch_shapes=[
+            pltpu.VMEM((n_all, width, WIDE), jnp.bfloat16),
+            pltpu.VMEM((utts, span, width), jnp.bfloat16),
+            pltpu.VMEM((WIDE // 256, utts, span + 2 * HALO, 128), jnp.float32),
+            pltpu.VMEM((n_in, utts, span, WIDE // 2), jnp.float32),
+            pltpu.VMEM((utts, span, width), jnp.bfloat16),
+            pltpu.SemaphoreType.DMA((n_all, 2)),
+            pltpu.SemaphoreType.DMA((n_all, 11)),
+            pltpu.SemaphoreType.DMA((n_all, 11)),
+        ],
+        compiler_params=pltpu.CompilerParams(
+            collective_id=0, has_side_effects=True, vmem_limit_bytes=60000000
+        ),
+    )(lengths, frames, norm_in_gain.reshape(1, -1), w_in, dw_kernel,
+      norm_mid_gain.reshape(1, -1), w_out)
+
+
 def solution(mesh):
+    paired = mesh.shape["fsdp"] == 8 and mesh.shape["dp"] % 2 == 0
     return jax.shard_map(
-        on_device,
+        fused_device if paired else on_device,
         mesh=mesh,
         in_specs=(
             P(("dp", "fsdp"), None, None),

time: 125 us -> 64 us (0.51)
  waiting for transfers between devices: 75.7 us -> 0 us
  Pallas kernels: 0 us -> 58.5 us
  other arithmetic: 19.1 us -> 0 us
  between operations: 13.5 us -> 0.01 us
  matrix products: 12.5 us -> 0 us
  local copies, waits for them, and re-layouts: 3.59 us -> 5.24 us
    all_gather x2 -> x0, waiting for transfers between devices: 74.3 us -> none  [the longest x1 57.6 us: expand_in(): lax.all_gather(w_in, 'fsdp', axis=0, tiled=True)]
    pallas_call x0 -> x1, Pallas kernels: none -> 58.5 us  [fused_device(): pl.pallas_call(fused_kernel, out_shape=jax.ShapeDtypeStruct(frames.shape,...]
    reduce_sum x4 -> x0, other arithmetic: 15.1 us -> none  [the longest x2 14.1 us: layer_norm(): center = values - jnp.mean(values, axis=-1, keepdims=True)]
    dot_general x2 -> x0, matrix products: 12.5 us -> none  [the longest x1 7.59 us: expand_in(): jnp.dot(flat_rows, lax.all_gather(w_in, 'fsdp', axis=0, tiled=True), pref...]
    slice x2 -> x0, local copies, waits for them, and re-layouts: 3.57 us -> none  [on_device(): dw_kernel[offset]]
    unnamed x8 -> x1, local copies, waits for them, and re-layouts: 0.02 us -> 2.65 us
    reshape x0 -> x2, local copies, waits for them, and re-layouts: none -> 2.58 us  [the longest x1 1.29 us: fused_device(): norm_in_gain.reshape(1, -1)]
    convert_element_type x3 -> x0, other arithmetic: 2.45 us -> none  [the longest x1 1.09 us: on_device(): middle = (middle * jax.nn.sigmoid(middle)).astype(jnp.bfloat16)]
  transfers between devices with their start and end apart: 2 -> 0, of which waited for: 2 -> 0; matrix products, arithmetic and copies ran while one was open for 23% -> 0% of each run, Pallas kernels for 0% -> 0%
where the time goes in v1:
time: 64 us; the launch traced here: 63.8 us
  Pallas kernels  58.5 us (91%)
  local copies, waits for them, and re-layouts  5.24 us (8%)
    pallas_call x1, Pallas kernels, fused_device(): pl.pallas_call(fused_kernel, out_shape=jax.ShapeDtypeStruct(frames.shape,...  58.5 us
    unnamed x1, local copies, waits for them, and re-layouts  2.65 us
    reshape x1, local copies, waits for them, and re-layouts, fused_device(): norm_in_gain.reshape(1, -1)  1.29 us
    reshape x1, local copies, waits for them, and re-layouts, fused_device(): norm_mid_gain.reshape(1, -1)  1.29 us

profile of v1, /device:TPU:0, one launch (start us, length us, event | category | flops | bytes accessed | tf_op | source)
XLA Modules:
  0.0 63.8 jit_solution(14058904649135428116)
XLA Ops:
  0.0 1.3 %reshape.6.gain_in = f32[1,1536]{1,0:T(1,128)} reshape(f32[1536]{0:T(1024)} %param.9) | data formatting | bytes 12288 | tf_op jit(solution)/shard_map/reshape | solution.py:317
  1.3 1.3 %reshape.7.gain_mid = f32[1,1536]{1,0:T(1,128)} reshape(f32[1536]{0:T(1024)} %param.12) | data formatting | bytes 12288 | tf_op jit(solution)/shard_map/reshape | solution.py:318
  2.6 58.5 %shard_map.73 = bf16[2,256,1536]{2,1,0:T(8,128)(2,1)} custom-call(s32[2]{0:T(128)} %lengths.1, bf16[2,256,1536]{2,1,0:T(8,128)(2,1)} %frames.1, f32[1,1536]{1,0:T(1,128)} %reshape.6.gain_in, bf16[192,3072]{1,0:T(8,128)(2,1)} %w_in.1, f32[31,1536]{1,0:T(8,128)} %taps.1, f32[1,1536]{1,0:T(1,128)} %reshape.7.gain_mid, bf16[192,1536]{1,0:T(8,128)(2,1)} %w_out.1), custom_call_target="tpu_custom_call" | custom-call | tf_op jit(solution)/shard_map/pallas_call | solution.py:299
  61.1 2.7 %copy.9 = bf16[2,256,1536]{2,1,0:T(8,128)(2,1)} copy(bf16[2,256,1536]{2,1,0:T(8,128)(2,1)} %shard_map.73) | data formatting | bytes 3145728

commit v2 on v1

--- a/solution.py
+++ b/solution.py
@@ -188,7 +188,7 @@
                 v = frames[u, at, :].astype(jnp.float32)
                 v = v - jnp.mean(v, axis=-1, keepdims=True)
                 var = jnp.mean(v * v, axis=-1, keepdims=True)
-                v = v * lax.rsqrt(var + 1e-05) * gain_in[...]
+                v = v * lax.rsqrt(var + 1e-05) * gain_in[...].reshape(1, width)
                 normed[u, at, :] = v.astype(jnp.bfloat16)
 
     def project(slot):
@@ -225,7 +225,7 @@
                 var = sum(jnp.sum(p * p, axis=-1, keepdims=True) for p in parts) / width
                 scale = lax.rsqrt(var + 1e-05)
                 for j, p in enumerate(parts):
-                    v = p * scale * gain_mid[:, j * cw:(j + 1) * cw]
+                    v = p * scale * gain_mid[j * cw:(j + 1) * cw].reshape(1, cw)
                     v = v * jax.nn.sigmoid(v)
                     middle[u, at, j * cw:(j + 1) * cw] = v.astype(jnp.bfloat16)
 
@@ -235,8 +235,7 @@
         to = pl.ds(pl.multiple_of((j - n_in) * WIDE, WIDE), WIDE)
         for u in range(utts):
             acc = jnp.dot(middle[u], wbuf[j], preferred_element_type=jnp.float32)
-            pos = lax.broadcasted_iota(jnp.int32, (span, WIDE), 0)
-            out[u, :, to] = jnp.where(pos < lengths[u], acc, 0.0).astype(jnp.bfloat16)
+            out[u, :, to] = acc.astype(jnp.bfloat16)
 
     m0, o0, s0, m1, o1, s1, m2, o2, s2 = range(n_all)
     for slot in (m0, s0, m1, o0, s1, m2, o1, s2, o2):
@@ -248,13 +247,13 @@
     pl.semaphore_wait(barrier, 4)
 
     own(m0)
+    own(s0)
     for lane in range(cw // 128):
         for u in range(utts):
             gated[lane, u, :HALO, :] = jnp.zeros((HALO, 128), jnp.float32)
             gated[lane, u, HALO + span:, :] = jnp.zeros((HALO, 128), jnp.float32)
     norm_in()
     relay(m0)
-    own(s0)
     finish(m0)
     own(m1)
     own(o0)
@@ -296,7 +295,7 @@
     n_all = n_in + width // WIDE
     vmem = pl.BlockSpec(memory_space=pltpu.VMEM)
     hbm = pl.BlockSpec(memory_space=pl.ANY)
-    return pl.pallas_call(
+    result = pl.pallas_call(
         fused_kernel,
         out_shape=jax.ShapeDtypeStruct(frames.shape, jnp.bfloat16),
         in_specs=[pl.BlockSpec(memory_space=pltpu.SMEM), vmem, vmem, hbm, vmem, vmem, hbm],
@@ -314,8 +313,10 @@
         compiler_params=pltpu.CompilerParams(
             collective_id=0, has_side_effects=True, vmem_limit_bytes=60000000
         ),
-    )(lengths, frames, norm_in_gain.reshape(1, -1), w_in, dw_kernel,
-      norm_mid_gain.reshape(1, -1), w_out)
+    )(lengths, frames, norm_in_gain, w_in, dw_kernel,
+      norm_mid_gain, w_out)
+    valid = jnp.arange(span, dtype=jnp.int32)[None, :] < lengths[:, None]
+    return jnp.where(valid[:, :, None], result, jnp.zeros((), jnp.bfloat16))
 
 
 def solution(mesh):

time: 64 us -> 61.5 us (0.961)
  local copies, waits for them, and re-layouts: 5.24 us -> 0 us
  other arithmetic: 0 us -> 3.45 us
    select_n x0 -> x1, other arithmetic: none -> 2.73 us  [fused_device(): return jnp.where(valid[:, :, None], result, jnp.zeros((), jnp.bfloat16))]
    unnamed x1 -> x0, local copies, waits for them, and re-layouts: 2.65 us -> none
    reshape x2 -> x0, local copies, waits for them, and re-layouts: 2.58 us -> none  [the longest x1 1.29 us: fused_device(): norm_in_gain.reshape(1, -1)]
    lt x0 -> x1, other arithmetic: none -> 0.73 us  [fused_device(): valid = jnp.arange(span, dtype=jnp.int32)[None, :] < lengths[:, None]]
where the time goes in v2:
time: 61.5 us; the launch traced here: 61.3 us
  Pallas kernels  57.9 us (94%)
  other arithmetic  3.45 us (6%)
    pallas_call x1, Pallas kernels, fused_device(): pl.pallas_call(fused_kernel, out_shape=jax.ShapeDtypeStruct(frames.shape,...  57.9 us
    select_n x1, other arithmetic, fused_device(): return jnp.where(valid[:, :, None], result, jnp.zeros((), jnp.bfloat16))  2.73 us

profile of v2, /device:TPU:0, one launch (start us, length us, event | category | flops | bytes accessed | tf_op | source)
XLA Modules:
  0.0 61.3 jit_solution(6971888538992419110)
XLA Ops:
  0.0 0.7 %iota_compare_fusion = pred[2,256]{1,0:T(4,128)(4,1)S(1)} fusion(s32[2]{0:T(128)} %lengths.1), kind=kLoop, calls=%fused_computation.1 | loop fusion | flops 512 | bytes 520 | tf_op jit(solution)/shard_map/lt | solution.py:318
  0.7 57.9 %shard_map.73 = bf16[2,256,1536]{2,1,0:T(8,128)(2,1)} custom-call(s32[2]{0:T(128)} %lengths.1, bf16[2,256,1536]{2,1,0:T(8,128)(2,1)} %frames.1, f32[1536]{0:T(1024)} %gain_in.1, bf16[192,3072]{1,0:T(8,128)(2,1)} %w_in.1, f32[31,1536]{1,0:T(8,128)} %taps.1, f32[1536]{0:T(1024)} %gain_mid.1, bf16[192,1536]{1,0:T(8,128)(2,1)} %w_out.1), custom_call_target="tpu_custom_call" | custom-call | tf_op jit(solution)/shard_map/pallas_call | solution.py:298
  58.6 2.7 %broadcast_select_fusion = bf16[2,256,1536]{2,1,0:T(8,128)(2,1)} fusion(bf16[2,256,1536]{2,1,0:T(8,128)(2,1)} %shard_map.73, pred[2,256]{1,0:T(4,128)(4,1)S(1)} %iota_compare_fusion), kind=kLoop, calls=%fused_computation | loop fusion | flops 786432 | bytes 3146240 | tf_op jit(solution)/shard_map/jit(_where)/select_n | solution.py:319
